TPU v7x, 32 devices: a whole 2x2x4 slice. The times are simulated.
32 devices in a mesh: own: 8 (over z, y), rep: 4 (over x, core).
Axes of the slice: x: 2, y: 2, z: 4, core: 2. Of those that a mesh axis runs over, the one named last changes fastest.
Arguments:
- hidden: bfloat16 [1024, 1024], P('own', 'rep'), may hold values from -140 to 140
- weight: bfloat16 [8, 2048, 1024], P('own', None, 'rep'), may hold values from -0.1875 to 0.1875
- bucket_map: int32 [8], replicated, may hold values from 0 to 7, each once
- active: int32 [1024, 2], P('own'), may hold values from 0 to 7, all different within a row; in each aligned block of 128 rows (0 to 127, 128 to 255, ...) at most 64 rows name the same one
- label_pick: int32 [1024], P('own'), may hold values from 0 to 4095
Outputs:
- sample_loss: float32 [1024], P('own')
- grad_hidden: float32 [1024, 1024], P('own', 'rep')
- grad_weight: bfloat16 [8, 2048, 1024], P('own', None, 'rep')
Inputs may be any that keep to these rules, and one draw needn't show every extreme that they name: `bucket_map`: each weight slot is named once. `active`: A sample's 2 bucket ids differ. Among the 128 samples of one index of own, no bucket is named by more than 64 samples, a bound that some block reaches.
All inputs are finite; a program needn't handle non-finite values.
Results may differ from a plain program's by a relative error of at most 0.0032.
Values may be sent and summed in bfloat16 or wider, within the bound.
A program may use at most 64 MiB of HBM per device.

v0:
```python
import jax
import jax.numpy as jnp
from jax import lax
from jax.sharding import PartitionSpec as P


def body(hidden, weight, bucket_map, active, label_pick):
    samp_count = hidden.shape[0]
    bucket_dev, label_count, feature_part = weight.shape
    picks = active.shape[1]
    bucket_total = bucket_map.shape[0]
    owner_count = lax.axis_size("own")
    slot_depth = max(2, 2 * samp_count * picks // bucket_total)
    pair_count = samp_count * picks
    slots_total = bucket_total * slot_depth
    row_count = owner_count * slot_depth
    pair_bucket = active.reshape(pair_count)
    bucket_iota = lax.broadcasted_iota(jnp.int32, (pair_count, bucket_total), 1)
    slot_index = jnp.sum(
        jnp.where(pair_bucket[:, None] == bucket_iota, bucket_map[None, :], 0), axis=1
    )
    slot_hits = (slot_index[:, None] == bucket_iota).astype(jnp.int32)
    earlier = jnp.cumsum(slot_hits, axis=0) - slot_hits
    rank_within = jnp.sum(earlier * slot_hits, axis=1)
    position = slot_index * slot_depth + rank_within
    pair_index = jnp.arange(pair_count, dtype=jnp.int32)
    pick_value = jnp.repeat(label_pick, picks)
    target_pair = jnp.where(
        pick_value // label_count == pair_index % picks, pick_value % label_count, -1
    )
    width_sent = hidden.shape[1]
    pair_rows = jnp.repeat(hidden, picks, axis=0)
    send_rows = jnp.zeros((slots_total, width_sent), jnp.bfloat16).at[position].set(pair_rows)
    send_target = jnp.full((slots_total,), -1, jnp.int32).at[position].set(target_pair)
    got_rows, got_target = (
        lax.all_to_all(
            send_rows.reshape(owner_count, bucket_dev * slot_depth, width_sent),
            "own",
            split_axis=0,
            concat_axis=0,
            tiled=True,
        ),
        lax.all_to_all(
            send_target.reshape(owner_count, bucket_dev * slot_depth),
            "own",
            split_axis=0,
            concat_axis=0,
            tiled=True,
        ),
    )
    received = got_rows.reshape(owner_count, bucket_dev, slot_depth, width_sent).transpose(
        1, 0, 2, 3
    )
    received = received.reshape(bucket_dev, row_count, width_sent)
    target_col = (
        got_target.reshape(owner_count, bucket_dev, slot_depth)
        .transpose(1, 0, 2)
        .reshape(bucket_dev, row_count)
    )
    partial_value = jnp.einsum("brd,bcd->brc", received, weight, preferred_element_type=jnp.float32)
    logits = lax.psum(partial_value, "rep")
    columns = lax.broadcasted_iota(jnp.int32, (1, 1, label_count), 2)
    row_max = jnp.max(logits, axis=2)
    row_sum = jnp.sum(jnp.exp(logits - row_max[..., None]), axis=2)
    row_target = jnp.sum(jnp.where(columns == target_col[..., None], logits, 0.0), axis=2)

    def to_sources(values):
        return (
            values.reshape(bucket_dev, owner_count, slot_depth)
            .transpose(1, 0, 2)
            .reshape(owner_count, bucket_dev * slot_depth)
        )

    back_max, back_sum, back_target = (
        lax.all_to_all(to_sources(row_max), "own", split_axis=0, concat_axis=0, tiled=True),
        lax.all_to_all(to_sources(row_sum), "own", split_axis=0, concat_axis=0, tiled=True),
        lax.all_to_all(to_sources(row_target), "own", split_axis=0, concat_axis=0, tiled=True),
    )
    pair_max = back_max.reshape(slots_total)[position].reshape(samp_count, picks)
    pair_sum = back_sum.reshape(slots_total)[position].reshape(samp_count, picks)
    pair_target = back_target.reshape(slots_total)[position].reshape(samp_count, picks)
    peak_max = jnp.max(pair_max, axis=1)
    norm_sum = jnp.sum(pair_sum * jnp.exp(pair_max - peak_max[:, None]), axis=1)
    log_norm = peak_max + jnp.log(norm_sum)
    sample_loss = log_norm - jnp.sum(pair_target, axis=1)
    send_norm = jnp.zeros((slots_total,), jnp.float32).at[position].set(jnp.repeat(log_norm, picks))
    got_norm = lax.all_to_all(
        send_norm.reshape(owner_count, bucket_dev * slot_depth),
        "own",
        split_axis=0,
        concat_axis=0,
        tiled=True,
    )
    row_norm = (
        got_norm.reshape(owner_count, bucket_dev, slot_depth)
        .transpose(1, 0, 2)
        .reshape(bucket_dev, row_count)
    )
    onehot = (columns == target_col[..., None]).astype(jnp.float32)
    grad_logits = (jnp.exp(logits - row_norm[..., None]) - onehot).astype(jnp.bfloat16)
    grad_weight = jnp.einsum(
        "brc,brd->bcd", grad_logits, received, preferred_element_type=jnp.float32
    ).astype(jnp.bfloat16)
    row_grads = jnp.einsum("brc,bcd->brd", grad_logits, weight, preferred_element_type=jnp.float32)
    send_grads = row_grads.reshape(bucket_dev, owner_count, slot_depth, feature_part).transpose(
        1, 0, 2, 3
    )
    send_grads = send_grads.reshape(owner_count, bucket_dev * slot_depth, feature_part)
    got_grads = lax.all_to_all(send_grads, "own", split_axis=0, concat_axis=0, tiled=True)
    pair_grads = got_grads.reshape(slots_total, feature_part)[position].reshape(
        samp_count, picks, feature_part
    )
    grad_hidden = jnp.sum(pair_grads, axis=1)
    return (sample_loss, grad_hidden, grad_weight)


def solution(mesh):
    in_specs = (P("own", "rep"), P("own", None, "rep"), P(), P("own", None), P("own"))
    out_specs = (P("own"), P("own", "rep"), P("own", None, "rep"))
    return jax.shard_map(body, mesh=mesh, in_specs=in_specs, out_specs=out_specs, check_vma=False)
```

profile of v0, /device:TPU:0, one launch (start us, length us, event | category | flops | bytes accessed | tf_op | source)
XLA Modules:
  0.0 201.0 jit_solution(17374603025491268575)
XLA Ops:
  7.2 0.9 copy.8
  8.1 0.1 eq.66
  8.2 0.7 select_reduce_fusion.1
  9.0 0.6 reduce-window.6
  9.6 0.2 slice_reduce_fusion
  9.9 0.9 broadcast_in_dim.50
  10.9 1.5 scatter_custom_fusion
  12.5 16.0 %all_to_all.55 = bf16[8,64,256]{2,1,0:T(8,128)(2,1)S(1)} all-to-all(bf16[8,64,256]{2,1,0:T(8,128)(2,1)S(1)} %bitcast.33), channel_id=1, replica_groups=mesh['own'=8,'rep'=4] {'own'}, dimensions={0} | all-to-all | bytes 524288 | tf_op jit(solution)/shard_map/all_to_all | solution.py:36
  28.5 2.7 %convolution_bitcast_fusion = f32[1,512,2048]{2,1,0:T(8,128)} fusion(bf16[512,256]{1,0:T(8,128)(2,1)S(1)} %bitcast.34, bf16[1,2048,256]{2,1,0:T(8,128)(2,1)S(1)} %copy-done), kind=kOutput, calls=%fused_computation.11 | convolution fusion | flops 536870912 | bytes 5505024 | tf_op jit(solution)/shard_map/brd,bcd->brc/dot_general | solution.py:60
  31.3 0.1 reshape.229
  31.5 1.4 scatter_custom_fusion.1
  32.9 9.8 %all_to_all.56 = s32[8,1,64]{2,1,0:T(1,128)S(1)} all-to-all(s32[8,1,64]{2,1,0:T(1,128)S(1)} %all_to_all.41), channel_id=1, replica_groups=mesh['own'=8,'rep'=4] {'own'}, dimensions={0} | all-to-all | bytes 4096 | tf_op jit(solution)/shard_map/all_to_all | solution.py:43
  42.8 0.5 broadcast.131
  43.3 0.7 reduce.22
  44.0 71.8 %all-reduce.2.cloned.1.call-done = f32[1,512,2048]{2,1,0:T(8,128)} async-done(((f32[1,512,2048]{2,1,0:T(8,128)}), f32[1,512,2048]{2,1,0:T(8,128)}) %all-reduce.2.cloned.1.call-update) | async-done | bytes 4194320 | tf_op jit(solution)/shard_map/psum | solution.py:61
  115.8 2.5 %reduce_max.18 = f32[512]{0:T(512)S(1)} reduce(f32[1,512,2048]{2,1,0:T(8,128)} %all-reduce.2.cloned.1.call-done, f32[]{:T(128)} %constant.50.clone.1), dimensions={0,2}, to_apply=%region_6.7 | reduce | flops 1048064 | bytes 4196356 | tf_op jit(solution)/shard_map/reduce_max | solution.py:63
  118.3 3.6 %select_reduce_fusion = (f32[512]{0:T(512)S(1)}, f32[512]{0:T(512)S(1)}) fusion(f32[1,512,2048]{2,1,0:T(8,128)} %all-reduce.2.cloned.1.call-done, s32[512]{0:T(512)S(1)} %eq.76, f32[512]{0:T(512)S(1)} %reduce_max.18), kind=kLoop, calls=%fused_computation.8 | loop fusion | flops 5241856 | bytes 4202496 | tf_op jit(solution)/shard_map/reduce_sum | solution.py:65
  121.9 0.7 all_to_all.39
  122.6 5.5 %all-to-all-start.2 = ((f32[8,1,64]{2,1,0:T(1,128)}), f32[8,1,64]{2,1,0:T(1,128)S(1)}, u32[]{:S(2)}, u32[]{:S(2)}) async-start(f32[8,1,64]{2,1,0:T(1,128)} %all_to_all.39), calls=%async_computation.2 | async-start | bytes 8192 | tf_op jit(solution)/shard_map/all_to_all | solution.py:76
  128.1 0.7 all_to_all.37
  128.8 5.7 %all-to-all-done.2 = f32[8,1,64]{2,1,0:T(1,128)S(1)} async-done(((f32[8,1,64]{2,1,0:T(1,128)}), f32[8,1,64]{2,1,0:T(1,128)S(1)}, u32[]{:S(2)}, u32[]{:S(2)}) %all-to-all-start.2) | async-done | bytes 2080 | tf_op jit(solution)/shard_map/all_to_all | solution.py:76
  134.5 3.3 %all-to-all-start.1 = ((f32[8,1,64]{2,1,0:T(1,128)}), f32[8,1,64]{2,1,0:T(1,128)S(1)}, u32[]{:S(2)}, u32[]{:S(2)}) async-start(f32[8,1,64]{2,1,0:T(1,128)} %all_to_all.37), calls=%async_computation.1 | async-start | bytes 8192 | tf_op jit(solution)/shard_map/all_to_all | solution.py:75
  137.8 0.7 all_to_all.43
  138.5 5.7 %all-to-all-done.1 = f32[8,1,64]{2,1,0:T(1,128)S(1)} async-done(((f32[8,1,64]{2,1,0:T(1,128)}), f32[8,1,64]{2,1,0:T(1,128)S(1)}, u32[]{:S(2)}, u32[]{:S(2)}) %all-to-all-start.1) | async-done | bytes 2080 | tf_op jit(solution)/shard_map/all_to_all | solution.py:75
  144.2 3.3 %all-to-all-start.4 = ((f32[8,1,64]{2,1,0:T(1,128)}), f32[8,1,64]{2,1,0:T(1,128)S(1)}, u32[]{:S(2)}, u32[]{:S(2)}) async-start(f32[8,1,64]{2,1,0:T(1,128)} %all_to_all.43), calls=%async_computation.4 | async-start | bytes 8192 | tf_op jit(solution)/shard_map/all_to_all | solution.py:77
  147.5 0.5 broadcast.129
  148.0 0.7 reduce.21
  148.7 1.9 gather_fusion.1
  150.7 0.1 reshape.228
  150.8 0.7 reduce.20
  151.6 1.9 gather_fusion
  153.8 0.7 reduce.23
  154.5 1.9 gather_fusion.2
  156.6 0.2 multiply_reduce_fusion
  156.9 0.5 fusion.14
  157.5 0.1 reshape.288
  157.7 1.4 scatter_custom_fusion.2
  159.2 12.2 %all_to_all.57 = f32[8,1,64]{2,1,0:T(1,128)S(1)} all-to-all(f32[8,1,64]{2,1,0:T(1,128)S(1)} %all_to_all.45), channel_id=1, replica_groups=mesh['own'=8,'rep'=4] {'own'}, dimensions={0} | all-to-all | bytes 4096 | tf_op jit(solution)/shard_map/all_to_all | solution.py:87
  171.4 0.7 reduce.24
  172.1 3.3 %subtract_convert_fusion = bf16[1,512,2048]{2,1,0:T(8,128)(2,1)S(1)} fusion(f32[1,512,2048]{2,1,0:T(8,128)} %all-reduce.2.cloned.1.call-done, f32[512]{0:T(512)S(1)} %sub.48, s32[512]{0:T(512)S(1)} %eq.76), kind=kLoop, calls=%fused_computation.7 | loop fusion | flops 5242880 | bytes 6295552 | tf_op jit(solution)/shard_map/convert_element_type | solution.py:100
  175.4 1.3 copy-done.1
  176.8 1.5 fusion.2
  178.3 3.5 %all-to-all-start.6 = ((f32[8,64,256]{2,1,0:T(8,128)}), f32[8,64,256]{2,1,0:T(8,128)S(1)}, u32[]{:S(2)}, u32[]{:S(2)}) async-start(f32[8,64,256]{2,1,0:T(8,128)} %fusion.2), calls=%async_computation.6 | async-start | bytes 1048576 | tf_op jit(solution)/shard_map/all_to_all | solution.py:109
  181.8 3.3 %fusion = bf16[1,2048,256]{2,1,0:T(8,128)(2,1)} fusion(bf16[512,256]{1,0:T(8,128)(2,1)S(1)} %bitcast.35, bf16[1,512,2048]{2,1,0:T(8,128)(2,1)} %copy-done.1), kind=kOutput, calls=%fused_computation.13 | convolution fusion | flops 537395200 | bytes 3407872 | tf_op jit(solution)/shard_map/brc,brd->bcd/dot_general | solution.py:101
  185.1 6.9 %all-to-all-done.6 = f32[8,64,256]{2,1,0:T(8,128)S(1)} async-done(((f32[8,64,256]{2,1,0:T(8,128)}), f32[8,64,256]{2,1,0:T(8,128)S(1)}, u32[]{:S(2)}, u32[]{:S(2)}) %all-to-all-start.6) | async-done | bytes 524320 | tf_op jit(solution)/shard_map/all_to_all | solution.py:109
  192.0 1.0 gather_fusion.3
  193.0 0.1 reshape.234
  193.2 1.0 reduce_sum.69
  (30 shorter events, 1.5 us)
Async XLA Ops:
  7.2 21.3 %copy-start = (bf16[1,2048,256]{2,1,0:T(8,128)(2,1)S(1)}, bf16[1,2048,256]{2,1,0:T(8,128)(2,1)}, u32[]{:S(2)}) copy-start(bf16[1,2048,256]{2,1,0:T(8,128)(2,1)} %param.6) | copy-start | bytes 3145732
  7.2 108.6 %all-reduce.2.cloned.1.call-start = ((), (), s32[]{:S(2)}) async-start(), calls=%async_computation.7 | async-start | bytes 8388608 | tf_op jit(solution)/shard_map/psum | solution.py:61
  28.5 2.7 %copy-start.2 = (s32[128]{0:T(128)S(1)}, s32[128]{0:T(128)}, u32[]{:S(2)}) copy-start(s32[128]{0:T(128)} %param.9) | copy-start | bytes 1540
  122.6 11.9 %all-to-all-start.2 = ((f32[8,1,64]{2,1,0:T(1,128)}), f32[8,1,64]{2,1,0:T(1,128)S(1)}, u32[]{:S(2)}, u32[]{:S(2)}) async-start(f32[8,1,64]{2,1,0:T(1,128)} %all_to_all.39), calls=%async_computation.2 | async-start | bytes 8192 | tf_op jit(solution)/shard_map/all_to_all | solution.py:76
  134.5 9.6 %all-to-all-start.1 = ((f32[8,1,64]{2,1,0:T(1,128)}), f32[8,1,64]{2,1,0:T(1,128)S(1)}, u32[]{:S(2)}, u32[]{:S(2)}) async-start(f32[8,1,64]{2,1,0:T(1,128)} %all_to_all.37), calls=%async_computation.1 | async-start | bytes 8192 | tf_op jit(solution)/shard_map/all_to_all | solution.py:75
  144.2 9.6 %all-to-all-start.4 = ((f32[8,1,64]{2,1,0:T(1,128)}), f32[8,1,64]{2,1,0:T(1,128)S(1)}, u32[]{:S(2)}, u32[]{:S(2)}) async-start(f32[8,1,64]{2,1,0:T(1,128)} %all_to_all.43), calls=%async_computation.4 | async-start | bytes 8192 | tf_op jit(solution)/shard_map/all_to_all | solution.py:77
  175.4 1.4 copy-start.1
  178.3 13.7 %all-to-all-start.6 = ((f32[8,64,256]{2,1,0:T(8,128)}), f32[8,64,256]{2,1,0:T(8,128)S(1)}, u32[]{:S(2)}, u32[]{:S(2)}) async-start(f32[8,64,256]{2,1,0:T(8,128)} %fusion.2), calls=%async_computation.6 | async-start | bytes 1048576 | tf_op jit(solution)/shard_map/all_to_all | solution.py:109
Sparse Core Ops, SparseCore 0:
  31.3 84.4 all-reduce.1
where the time goes:
time: 202 us; the launch traced here: 201 us
  waiting for transfers between devices  90.1 us (45%)
  blocking collectives  38 us (19%)
  local copies, waits for them, and re-layouts  19.3 us (10%)
  other arithmetic  16.1 us (8%)
  starting transfers between devices  15.7 us (8%)
  between operations  14.3 us (7%)
  matrix products  7.55 us (4%)
    psum x1, waiting for transfers between devices, body(): logits = lax.psum(partial_value, 'rep')  71.8 us
    all_to_all x1, blocking collectives, body(): lax.all_to_all(send_rows.reshape(owner_count, bucket_dev * slot_depth, wi...  16 us
    all_to_all x1, blocking collectives, body(): lax.all_to_all(send_norm.reshape(owner_count, bucket_dev * slot_depth), '...  12.2 us
    all_to_all x1, blocking collectives, body(): lax.all_to_all(send_target.reshape(owner_count, bucket_dev * slot_depth),...  9.84 us
    all_to_all x1, waiting for transfers between devices, body(): lax.all_to_all(send_grads, 'own', split_axis=0, concat_axis=0, tiled=True)  6.92 us
    all_to_all x1, waiting for transfers between devices, body(): lax.all_to_all(to_sources(row_sum), 'own', split_axis=0, concat_axis=0, t...  5.72 us
    all_to_all x1, waiting for transfers between devices, body(): lax.all_to_all(to_sources(row_max), 'own', split_axis=0, concat_axis=0, t...  5.65 us
    all_to_all x1, starting transfers between devices, body(): lax.all_to_all(to_sources(row_sum), 'own', split_axis=0, concat_axis=0, t...  5.52 us
  transfers between devices with their start and end apart: 5, of which 4 were waited for; matrix products, arithmetic and copies ran while one was open for 6% of the time, Pallas kernels for 0%

commit v1 on v0

--- a/solution.py
+++ b/solution.py
@@ -2,6 +2,7 @@
 import jax.numpy as jnp
 from jax import lax
 from jax.sharding import PartitionSpec as P
+from jax.lax import all_gather
 
 
 def body(hidden, weight, bucket_map, active, label_pick):
@@ -58,7 +59,12 @@
         .reshape(bucket_dev, row_count)
     )
     partial_value = jnp.einsum("brd,bcd->brc", received, weight, preferred_element_type=jnp.float32)
-    logits = lax.psum(partial_value, "rep")
+
+    def chains_lift(u, a_name):
+        now = jnp.sum(all_gather(u, a_name), axis=0)
+        return now
+
+    logits = chains_lift(partial_value, "rep")
     columns = lax.broadcasted_iota(jnp.int32, (1, 1, label_count), 2)
     row_max = jnp.max(logits, axis=2)
     row_sum = jnp.sum(jnp.exp(logits - row_max[..., None]), axis=2)

time: 202 us -> 231 us (1.14)
  waiting for transfers between devices: 90.1 us -> 110 us
  other arithmetic: 16.1 us -> 26.2 us
    all_gather x0 -> x1, waiting for transfers between devices: none -> 92.2 us  [chains_lift(): now = jnp.sum(all_gather(u, a_name), axis=0)]
    psum x1 -> x0, waiting for transfers between devices: 71.8 us -> none  [body(): logits = lax.psum(partial_value, 'rep')]
    reduce_sum x0 -> x1, other arithmetic: none -> 10.1 us  [chains_lift(): now = jnp.sum(all_gather(u, a_name), axis=0)]
where the time goes in v1:
time: 231 us
  waiting for transfers between devices  110 us (48%)
  blocking collectives  38 us (16%)
  other arithmetic  26.2 us (11%)
  local copies, waits for them, and re-layouts  17.9 us (8%)
  starting transfers between devices  15.7 us (7%)
  between operations  14.3 us (6%)
  matrix products  8.91 us (4%)
    all_gather x1, waiting for transfers between devices, chains_lift(): now = jnp.sum(all_gather(u, a_name), axis=0)  92.2 us
    all_to_all x1, blocking collectives, body(): lax.all_to_all(send_rows.reshape(owner_count, bucket_dev * slot_depth, wi...  16 us
    all_to_all x1, blocking collectives, body(): lax.all_to_all(send_norm.reshape(owner_count, bucket_dev * slot_depth), '...  12.2 us
    reduce_sum x1, other arithmetic, chains_lift(): now = jnp.sum(all_gather(u, a_name), axis=0)  10.1 us
    all_to_all x1, blocking collectives, body(): lax.all_to_all(send_target.reshape(owner_count, bucket_dev * slot_depth),...  9.84 us
    all_to_all x1, waiting for transfers between devices, body(): lax.all_to_all(send_grads, 'own', split_axis=0, concat_axis=0, tiled=True)  6.07 us
    all_to_all x1, waiting for transfers between devices, body(): lax.all_to_all(to_sources(row_sum), 'own', split_axis=0, concat_axis=0, t...  5.72 us
    all_to_all x1, waiting for transfers between devices, body(): lax.all_to_all(to_sources(row_max), 'own', split_axis=0, concat_axis=0, t...  5.65 us
  transfers between devices with their start and end apart: 5, of which 4 were waited for; matrix products, arithmetic and copies ran while one was open for 6% of the time, Pallas kernels for 0%

profile of v1, /device:TPU:0, one launch (start us, length us, event | category | flops | bytes accessed | tf_op | source)
XLA Modules:
  0.0 230.7 jit_solution(2563021903725055692)
XLA Ops:
  7.2 0.9 copy.8
  8.1 0.1 eq.88
  8.2 0.7 select_reduce_fusion.1
  9.0 0.6 reduce-window.6
  9.6 0.2 slice_reduce_fusion
  9.9 0.9 broadcast_in_dim.50
  10.9 1.5 scatter_custom_fusion
  12.5 16.0 %all_to_all.55 = bf16[8,64,256]{2,1,0:T(8,128)(2,1)S(1)} all-to-all(bf16[8,64,256]{2,1,0:T(8,128)(2,1)S(1)} %bitcast.44), channel_id=1, replica_groups=mesh['own'=8,'rep'=4] {'own'}, dimensions={0} | all-to-all | bytes 524288 | tf_op jit(solution)/shard_map/all_to_all | solution.py:37
  28.5 2.7 %fusion.10 = f32[512,2048]{1,0:T(8,128)} fusion(bf16[512,256]{1,0:T(8,128)(2,1)S(1)} %bitcast.45, bf16[1,2048,256]{2,1,0:T(8,128)(2,1)S(1)} %copy-done), kind=kOutput, calls=%fused_computation.23 | convolution fusion | flops 536870912 | bytes 5505024 | tf_op jit(solution)/shard_map/brd,bcd->brc/dot_general | solution.py:61
  31.2 0.1 reshape.383
  31.4 1.4 scatter_custom_fusion.1
  32.9 9.8 %all_to_all.56 = s32[8,1,64]{2,1,0:T(1,128)S(1)} all-to-all(s32[8,1,64]{2,1,0:T(1,128)S(1)} %all_to_all.41), channel_id=1, replica_groups=mesh['own'=8,'rep'=4] {'own'}, dimensions={0} | all-to-all | bytes 4096 | tf_op jit(solution)/shard_map/all_to_all | solution.py:44
  42.7 0.5 broadcast.183
  43.2 0.7 reduce.28
  44.0 92.2 %all-gather.3.cloned.1.call-done = f32[2048,2048]{1,0:T(8,128)} async-done(((f32[512,2048]{1,0:T(8,128)}), f32[2048,2048]{1,0:T(8,128)}) %all-gather.3.cloned.1.call-update) | async-done | bytes 16777232 | tf_op jit(solution)/shard_map/all_gather | solution.py:64
  136.2 10.1 %reduce.7 = f32[512,2048]{1,0:T(8,128)} reduce(f32[4,512,2048]{2,1,0:T(8,128)} %bitcast.41, f32[]{:T(128)} %constant.50.clone.1), dimensions={0}, to_apply=%region_5.6 | reduce | flops 3145728 | bytes 20971524 | tf_op jit(solution)/shard_map/reduce_sum | solution.py:64
  146.3 2.5 %reduce_max.18 = f32[512]{0:T(512)S(1)} reduce(f32[512,2048]{1,0:T(8,128)} %reduce.7, f32[]{:T(128)} %constant.51.clone.1), dimensions={1}, to_apply=%region_6.7 | reduce | flops 1048064 | bytes 4196356 | tf_op jit(solution)/shard_map/reduce_max | solution.py:69
  148.8 3.6 %select_reduce_fusion = (f32[512]{0:T(512)S(1)}, f32[512]{0:T(512)S(1)}) fusion(f32[512,2048]{1,0:T(8,128)} %reduce.7, s32[512]{0:T(512)S(1)} %eq.98, f32[512]{0:T(512)S(1)} %reduce_max.18), kind=kLoop, calls=%fused_computation.13 | loop fusion | flops 5241856 | bytes 4202496 | tf_op jit(solution)/shard_map/reduce_sum | solution.py:71
  152.4 0.7 all_to_all.39
  153.1 5.5 %all-to-all-start.2 = ((f32[8,1,64]{2,1,0:T(1,128)}), f32[8,1,64]{2,1,0:T(1,128)S(1)}, u32[]{:S(2)}, u32[]{:S(2)}) async-start(f32[8,1,64]{2,1,0:T(1,128)} %all_to_all.39), calls=%async_computation.2 | async-start | bytes 8192 | tf_op jit(solution)/shard_map/all_to_all | solution.py:82
  158.6 0.7 all_to_all.37
  159.3 5.7 %all-to-all-done.2 = f32[8,1,64]{2,1,0:T(1,128)S(1)} async-done(((f32[8,1,64]{2,1,0:T(1,128)}), f32[8,1,64]{2,1,0:T(1,128)S(1)}, u32[]{:S(2)}, u32[]{:S(2)}) %all-to-all-start.2) | async-done | bytes 2080 | tf_op jit(solution)/shard_map/all_to_all | solution.py:82
  165.0 3.3 %all-to-all-start.1 = ((f32[8,1,64]{2,1,0:T(1,128)}), f32[8,1,64]{2,1,0:T(1,128)S(1)}, u32[]{:S(2)}, u32[]{:S(2)}) async-start(f32[8,1,64]{2,1,0:T(1,128)} %all_to_all.37), calls=%async_computation.1 | async-start | bytes 8192 | tf_op jit(solution)/shard_map/all_to_all | solution.py:81
  168.3 0.7 all_to_all.43
  169.0 5.7 %all-to-all-done.1 = f32[8,1,64]{2,1,0:T(1,128)S(1)} async-done(((f32[8,1,64]{2,1,0:T(1,128)}), f32[8,1,64]{2,1,0:T(1,128)S(1)}, u32[]{:S(2)}, u32[]{:S(2)}) %all-to-all-start.1) | async-done | bytes 2080 | tf_op jit(solution)/shard_map/all_to_all | solution.py:81
  174.7 3.3 %all-to-all-start.4 = ((f32[8,1,64]{2,1,0:T(1,128)}), f32[8,1,64]{2,1,0:T(1,128)S(1)}, u32[]{:S(2)}, u32[]{:S(2)}) async-start(f32[8,1,64]{2,1,0:T(1,128)} %all_to_all.43), calls=%async_computation.4 | async-start | bytes 8192 | tf_op jit(solution)/shard_map/all_to_all | solution.py:83
  178.0 0.5 broadcast.181
  178.5 0.7 reduce.27
  179.3 1.9 gather_fusion.1
  181.2 0.1 reshape.382
  181.3 0.7 reduce.26
  182.1 1.9 gather_fusion
  184.3 0.7 reduce.29
  185.1 1.9 gather_fusion.2
  187.3 0.2 multiply_reduce_fusion
  187.4 0.5 fusion.21
  188.1 0.1 reshape.441
  188.2 1.4 scatter_custom_fusion.2
  189.7 12.2 %all_to_all.57 = f32[8,1,64]{2,1,0:T(1,128)S(1)} all-to-all(f32[8,1,64]{2,1,0:T(1,128)S(1)} %all_to_all.45), channel_id=1, replica_groups=mesh['own'=8,'rep'=4] {'own'}, dimensions={0} | all-to-all | bytes 4096 | tf_op jit(solution)/shard_map/all_to_all | solution.py:93
  201.9 0.7 reduce.30
  202.6 3.3 %subtract_convert_fusion = bf16[512,2048]{1,0:T(8,128)(2,1)S(1)} fusion(f32[512,2048]{1,0:T(8,128)} %reduce.7, f32[512]{0:T(512)S(1)} %sub.109, s32[512]{0:T(512)S(1)} %eq.98), kind=kLoop, calls=%fused_computation.12 | loop fusion | flops 5242880 | bytes 6295552 | tf_op jit(solution)/shard_map/convert_element_type | solution.py:106
  205.9 1.5 fusion.8
  207.4 3.5 %all-to-all-start.6 = ((f32[8,64,256]{2,1,0:T(8,128)}), f32[8,64,256]{2,1,0:T(8,128)S(1)}, u32[]{:S(2)}, u32[]{:S(2)}) async-start(f32[8,64,256]{2,1,0:T(8,128)} %fusion.8), calls=%async_computation.6 | async-start | bytes 1048576 | tf_op jit(solution)/shard_map/all_to_all | solution.py:115
  210.9 4.7 %fusion.3 = bf16[1,2048,256]{2,1,0:T(8,128)(2,1)} fusion(bf16[512,256]{1,0:T(8,128)(2,1)S(1)} %bitcast.46, f32[512,2048]{1,0:T(8,128)} %reduce.7, s32[512]{0:T(512)S(1)} %eq.98, f32[512]{0:T(512)S(1)} %sub.109), kind=kOutput, calls=%fused_computation.17 | convolution fusion | flops 542638080 | bytes 5509120 | tf_op jit(solution)/shard_map/brc,brd->bcd/dot_general | solution.py:107
  215.7 6.1 %all-to-all-done.6 = f32[8,64,256]{2,1,0:T(8,128)S(1)} async-done(((f32[8,64,256]{2,1,0:T(8,128)}), f32[8,64,256]{2,1,0:T(8,128)S(1)}, u32[]{:S(2)}, u32[]{:S(2)}) %all-to-all-start.6) | async-done | bytes 524320 | tf_op jit(solution)/shard_map/all_to_all | solution.py:115
  221.8 1.0 gather_fusion.3
  222.7 0.1 reshape.388
  222.9 1.0 reduce_sum.81
  (29 shorter events, 1.5 us)
Async XLA Ops:
  7.2 21.3 %copy-start = (bf16[1,2048,256]{2,1,0:T(8,128)(2,1)S(1)}, bf16[1,2048,256]{2,1,0:T(8,128)(2,1)}, u32[]{:S(2)}) copy-start(bf16[1,2048,256]{2,1,0:T(8,128)(2,1)} %param.6) | copy-start | bytes 3145732
  7.2 129.1 %all-gather.3.cloned.1.call-start = ((), (), s32[]{:S(2)}) async-start(), calls=%async_computation.7 | async-start | bytes 20971520 | tf_op jit(solution)/shard_map/all_gather | solution.py:64
  28.5 2.7 %copy-start.1 = (s32[128]{0:T(128)S(1)}, s32[128]{0:T(128)}, u32[]{:S(2)}) copy-start(s32[128]{0:T(128)} %param.9) | copy-start | bytes 1540
  153.1 11.9 %all-to-all-start.2 = ((f32[8,1,64]{2,1,0:T(1,128)}), f32[8,1,64]{2,1,0:T(1,128)S(1)}, u32[]{:S(2)}, u32[]{:S(2)}) async-start(f32[8,1,64]{2,1,0:T(1,128)} %all_to_all.39), calls=%async_computation.2 | async-start | bytes 8192 | tf_op jit(solution)/shard_map/all_to_all | solution.py:82
  165.0 9.6 %all-to-all-start.1 = ((f32[8,1,64]{2,1,0:T(1,128)}), f32[8,1,64]{2,1,0:T(1,128)S(1)}, u32[]{:S(2)}, u32[]{:S(2)}) async-start(f32[8,1,64]{2,1,0:T(1,128)} %all_to_all.37), calls=%async_computation.1 | async-start | bytes 8192 | tf_op jit(solution)/shard_map/all_to_all | solution.py:81
  174.7 9.6 %all-to-all-start.4 = ((f32[8,1,64]{2,1,0:T(1,128)}), f32[8,1,64]{2,1,0:T(1,128)S(1)}, u32[]{:S(2)}, u32[]{:S(2)}) async-start(f32[8,1,64]{2,1,0:T(1,128)} %all_to_all.43), calls=%async_computation.4 | async-start | bytes 8192 | tf_op jit(solution)/shard_map/all_to_all | solution.py:83
  207.4 14.3 %all-to-all-start.6 = ((f32[8,64,256]{2,1,0:T(8,128)}), f32[8,64,256]{2,1,0:T(8,128)S(1)}, u32[]{:S(2)}, u32[]{:S(2)}) async-start(f32[8,64,256]{2,1,0:T(8,128)} %fusion.8), calls=%async_computation.6 | async-start | bytes 1048576 | tf_op jit(solution)/shard_map/all_to_all | solution.py:115
Sparse Core Ops, SparseCore 0:
  31.3 104.9 all-gather.2
